TPU v7x, 512 devices: a whole 4x8x8 slice. The times are simulated.
512 devices in a mesh: slab: 64 (over x, y, z_lo), col: 8 (over z_hi, core).
Axes of the slice: x: 4, y: 8, z: 8 (z_hi: 4, z_lo: 2; z = z_hi * 2 + z_lo), core: 2. Of those that a mesh axis runs over, the one named last changes fastest.
Arguments:
- green_blocks: float32 [64, 2, 2048, 2048], P('slab', None, None, 'col'), may hold values from -0.125 to 0.125
- traces: float32 [64, 2, 64, 2048], P('slab', None, None, 'col'), may hold values from -6 to 6
- sources: float32 [64, 2, 64, 2048], P('slab', None, None, 'col'), may hold values from -6 to 6
Outputs:
- swept: float32 [64, 2, 64, 2048], P('slab', None, None, 'col')
All inputs are finite; a program needn't handle non-finite values.
Results may differ from a plain program's by a relative error of at most 0.00014.
Values sent between devices are 32-bit elements; how exact they have to be, the bound alone decides.
A program may use at most 64 MiB of HBM per device.

v0:
```python
import jax
import jax.numpy as jnp
from jax import lax
from jax.sharding import PartitionSpec as P

STEPS = 4


def from_behind(block, axis, distance):
    devices = range(lax.axis_size(axis))
    route = [(i - distance, i) for i in devices if i - distance in devices]
    return lax.ppermute(block, axis, route)


def matmul_t(left, right):
    return lax.dot_general(
        left,
        right,
        (((1,), (1,)), ((), ())),
        precision=lax.Precision.HIGHEST,
        preferred_element_type=jnp.float32,
    )


def pass_down(current):
    return from_behind(current, "slab", 1)


def complex_apply(real_mat, imag_mat, real_vec, imag_vec):
    real_out = matmul_t(real_vec, real_mat) - matmul_t(imag_vec, imag_mat)
    imag_out = matmul_t(imag_vec, real_mat) + matmul_t(real_vec, imag_mat)
    return jnp.stack([real_out, imag_out], 0)


def shards(green_blocks, traces, sources):
    current = traces
    for step_index in range(STEPS):
        from_above = pass_down(current)
        partial_value = complex_apply(
            green_blocks[0, 0], green_blocks[0, 1], from_above[0, 0], from_above[0, 1]
        )[None]
        current = lax.psum_scatter(partial_value, "col", scatter_dimension=3, tiled=True) + sources
    return current


def solution(mesh):
    placed = (
        P("slab", None, None, "col"),
        P("slab", None, None, "col"),
        P("slab", None, None, "col"),
    )
    return jax.shard_map(
        shards, mesh=mesh, in_specs=placed, out_specs=P("slab", None, None, "col"), check_vma=False
    )
```

profile of v0, /device:TPU:7, one launch (start us, length us, event | category | flops | bytes accessed | tf_op | source)
XLA Modules:
  0.0 273.7 jit_solution(3512092833506498618)
XLA Ops:
  6.5 0.0 reduce-scatter.5.cloned.1.call-start
  6.5 0.0 copy-start
  6.5 4.3 %collective-permute-start = (f32[1,2,64,256]{3,2,1,0:T(8,128)}, f32[1,2,64,256]{3,2,1,0:T(8,128)S(1)}, u32[]{:S(2)}, u32[]{:S(2)}) collective-permute-start(f32[1,2,64,256]{3,2,1,0:T(8,128)} %param.4), channel_id=1, source_target_pairs={{0,8},{8,16},{16,24},{24,32},{32,40},{40,48},{48,56},{56,64},{64,7... | collective-permute-start | bytes 393224 | tf_op jit(solution)/shard_map/ppermute | solution.py:12
  10.8 6.6 %collective-permute-done = f32[1,2,64,256]{3,2,1,0:T(8,128)S(1)} collective-permute-done((f32[1,2,64,256]{3,2,1,0:T(8,128)}, f32[1,2,64,256]{3,2,1,0:T(8,128)S(1)}, u32[]{:S(2)}, u32[]{:S(2)}) %collective-permute-start) | collective-permute-done | bytes 131104 | tf_op jit(solution)/shard_map/ppermute | solution.py:12
  17.4 3.7 %fusion.20 = f32[64,2048]{1,0:T(8,128)S(1)} fusion(f32[1,2,2048,256]{3,2,1,0:T(8,128)} %param.3, f32[1,2,64,256]{3,2,1,0:T(8,128)S(1)} %collective-permute-done), kind=kOutput, calls=%fused_computation.28 | convolution fusion | flops 402653184 | bytes 2686976 | tf_op jit(solution)/shard_map/dot_general | solution.py:16
  21.1 3.7 %fusion.22 = f32[64,2048]{1,0:T(8,128)S(1)} fusion(f32[1,2,2048,256]{3,2,1,0:T(8,128)} %param.3, f32[1,2,64,256]{3,2,1,0:T(8,128)S(1)} %collective-permute-done), kind=kOutput, calls=%fused_computation.30 | convolution fusion | flops 402653184 | bytes 2686976 | tf_op jit(solution)/shard_map/dot_general | solution.py:16
  24.7 0.0 copy-done
  24.8 0.0 copy-start.4
  24.8 2.1 fusion.1
  26.9 2.1 fusion
  29.0 1.0 maximum_bitcast_fusion
  30.1 0.0 reduce-scatter.5.cloned.1.call-update
  30.1 0.0 reduce-scatter.7.cloned.1.call-start
  30.1 45.2 %reduce-scatter.5.cloned.1.call-done = f32[1,2,64,256]{3,2,1,0:T(8,128)} async-done(((f32[1,2,64,2048]{3,2,1,0:T(8,128)}), f32[1,2,64,256]{3,2,1,0:T(8,128)}) %reduce-scatter.5.cloned.1.call-update) | async-done | bytes 131088 | tf_op jit(solution)/shard_map/reduce_scatter | solution.py:42
  75.3 0.0 copy-done.4
  75.3 0.0 copy-start.1
  75.3 1.1 add.33
  76.4 2.2 collective-permute-start.1
  78.6 6.6 %collective-permute-done.1 = f32[1,2,64,256]{3,2,1,0:T(8,128)S(1)} collective-permute-done((f32[1,2,64,256]{3,2,1,0:T(8,128)S(1)}, f32[1,2,64,256]{3,2,1,0:T(8,128)S(1)}, u32[]{:S(2)}, u32[]{:S(2)}) %collective-permute-start.1) | collective-permute-done | bytes 131104 | tf_op jit(solution)/shard_map/ppermute | solution.py:12
  85.2 3.7 %fusion.16 = f32[64,2048]{1,0:T(8,128)S(1)} fusion(f32[1,2,2048,256]{3,2,1,0:T(8,128)} %param.3, f32[1,2,64,256]{3,2,1,0:T(8,128)S(1)} %collective-permute-done.1), kind=kOutput, calls=%fused_computation.24 | convolution fusion | flops 402653184 | bytes 2686976 | tf_op jit(solution)/shard_map/dot_general | solution.py:16
  88.9 3.7 %fusion.18 = f32[64,2048]{1,0:T(8,128)S(1)} fusion(f32[1,2,2048,256]{3,2,1,0:T(8,128)} %param.3, f32[1,2,64,256]{3,2,1,0:T(8,128)S(1)} %collective-permute-done.1), kind=kOutput, calls=%fused_computation.26 | convolution fusion | flops 402653184 | bytes 2686976 | tf_op jit(solution)/shard_map/dot_general | solution.py:16
  92.6 0.0 copy-done.1
  92.6 2.1 fusion.3
  94.7 2.1 fusion.2
  96.8 1.0 maximum_bitcast_fusion.1
  97.9 0.0 reduce-scatter.7.cloned.1.call-update
  97.9 0.0 reduce-scatter.9.cloned.1.call-start
  98.0 40.8 %reduce-scatter.7.cloned.1.call-done = f32[1,2,64,256]{3,2,1,0:T(8,128)} async-done(((f32[1,2,64,2048]{3,2,1,0:T(8,128)}), f32[1,2,64,256]{3,2,1,0:T(8,128)}) %reduce-scatter.7.cloned.1.call-update) | async-done | bytes 131088 | tf_op jit(solution)/shard_map/reduce_scatter | solution.py:42
  138.7 0.0 copy-start.2
  138.7 1.1 add.35
  139.8 2.4 collective-permute-start.2
  142.2 6.5 %collective-permute-done.2 = f32[1,2,64,256]{3,2,1,0:T(8,128)S(1)} collective-permute-done((f32[1,2,64,256]{3,2,1,0:T(8,128)S(1)}, f32[1,2,64,256]{3,2,1,0:T(8,128)S(1)}, u32[]{:S(2)}, u32[]{:S(2)}) %collective-permute-start.2) | collective-permute-done | bytes 131104 | tf_op jit(solution)/shard_map/ppermute | solution.py:12
  148.7 3.7 %fusion.12 = f32[64,2048]{1,0:T(8,128)S(1)} fusion(f32[1,2,2048,256]{3,2,1,0:T(8,128)} %param.3, f32[1,2,64,256]{3,2,1,0:T(8,128)S(1)} %collective-permute-done.2), kind=kOutput, calls=%fused_computation.20 | convolution fusion | flops 402653184 | bytes 2686976 | tf_op jit(solution)/shard_map/dot_general | solution.py:16
  152.3 3.7 %fusion.14 = f32[64,2048]{1,0:T(8,128)S(1)} fusion(f32[1,2,2048,256]{3,2,1,0:T(8,128)} %param.3, f32[1,2,64,256]{3,2,1,0:T(8,128)S(1)} %collective-permute-done.2), kind=kOutput, calls=%fused_computation.22 | convolution fusion | flops 402653184 | bytes 2686976 | tf_op jit(solution)/shard_map/dot_general | solution.py:16
  156.0 0.0 copy-done.2
  156.0 2.1 fusion.5
  158.2 2.1 fusion.4
  160.3 1.0 maximum_bitcast_fusion.2
  161.3 0.0 reduce-scatter.9.cloned.1.call-update
  161.3 0.0 reduce-scatter.11.cloned.1.call-start
  161.4 40.8 %reduce-scatter.9.cloned.1.call-done = f32[1,2,64,256]{3,2,1,0:T(8,128)} async-done(((f32[1,2,64,2048]{3,2,1,0:T(8,128)}), f32[1,2,64,256]{3,2,1,0:T(8,128)}) %reduce-scatter.9.cloned.1.call-update) | async-done | bytes 131088 | tf_op jit(solution)/shard_map/reduce_scatter | solution.py:42
  202.2 0.0 copy-start.3
  202.2 1.1 add.37
  203.3 2.3 collective-permute-start.3
  205.6 6.5 %collective-permute-done.3 = f32[1,2,64,256]{3,2,1,0:T(8,128)S(1)} collective-permute-done((f32[1,2,64,256]{3,2,1,0:T(8,128)S(1)}, f32[1,2,64,256]{3,2,1,0:T(8,128)S(1)}, u32[]{:S(2)}, u32[]{:S(2)}) %collective-permute-start.3) | collective-permute-done | bytes 131104 | tf_op jit(solution)/shard_map/ppermute | solution.py:12
  212.2 3.7 %fusion.8 = f32[64,2048]{1,0:T(8,128)S(1)} fusion(f32[1,2,2048,256]{3,2,1,0:T(8,128)} %param.3, f32[1,2,64,256]{3,2,1,0:T(8,128)S(1)} %collective-permute-done.3), kind=kOutput, calls=%fused_computation.16 | convolution fusion | flops 402653184 | bytes 2686976 | tf_op jit(solution)/shard_map/dot_general | solution.py:16
  215.9 3.7 %fusion.10 = f32[64,2048]{1,0:T(8,128)S(1)} fusion(f32[1,2,2048,256]{3,2,1,0:T(8,128)} %param.3, f32[1,2,64,256]{3,2,1,0:T(8,128)S(1)} %collective-permute-done.3), kind=kOutput, calls=%fused_computation.18 | convolution fusion | flops 402653184 | bytes 2686976 | tf_op jit(solution)/shard_map/dot_general | solution.py:16
  219.5 0.0 copy-done.3
  219.6 2.1 fusion.7
  221.7 2.1 fusion.6
  223.8 1.0 maximum_bitcast_fusion.3
  224.8 0.0 reduce-scatter.11.cloned.1.call-update
  224.9 40.8 %reduce-scatter.11.cloned.1.call-done = f32[1,2,64,256]{3,2,1,0:T(8,128)} async-done(((f32[1,2,64,2048]{3,2,1,0:T(8,128)}), f32[1,2,64,256]{3,2,1,0:T(8,128)}) %reduce-scatter.11.cloned.1.call-update) | async-done | bytes 131088 | tf_op jit(solution)/shard_map/reduce_scatter | solution.py:42
  265.6 1.6 add.39
Async XLA Ops:
  6.5 68.8 %reduce-scatter.5.cloned.1.call-start = ((), (), s32[]{:S(2)}) async-start(), calls=%async_computation.4 | async-start | bytes 1179648 | tf_op jit(solution)/shard_map/reduce_scatter | solution.py:42
  6.5 18.2 %copy-start = (f32[1,2,2048,256]{3,2,1,0:T(8,128)S(1)}, f32[1,2,2048,256]{3,2,1,0:T(8,128)}, u32[]{:S(2)}) copy-start(f32[1,2,2048,256]{3,2,1,0:T(8,128)} %param.3) | copy-start | bytes 12582916
  6.5 10.8 %collective-permute-start = (f32[1,2,64,256]{3,2,1,0:T(8,128)}, f32[1,2,64,256]{3,2,1,0:T(8,128)S(1)}, u32[]{:S(2)}, u32[]{:S(2)}) collective-permute-start(f32[1,2,64,256]{3,2,1,0:T(8,128)} %param.4), channel_id=1, source_target_pairs={{0,8},{8,16},{16,24},{24,32},{32,40},{40,48},{48,56},{56,64},{64,7... | collective-permute-start | bytes 393224 | tf_op jit(solution)/shard_map/ppermute | solution.py:12
  24.8 50.5 %copy-start.4 = (f32[1,2,64,256]{3,2,1,0:T(8,128)S(1)}, f32[1,2,64,256]{3,2,1,0:T(8,128)}, u32[]{:S(2)}) copy-start(f32[1,2,64,256]{3,2,1,0:T(8,128)} %param.5) | copy-start | bytes 393220
  30.1 108.7 %reduce-scatter.7.cloned.1.call-start = ((), (), s32[]{:S(2)}) async-start(), calls=%async_computation.5 | async-start | bytes 1179648 | tf_op jit(solution)/shard_map/reduce_scatter | solution.py:42
  75.3 17.3 %copy-start.1 = (f32[1,2,2048,256]{3,2,1,0:T(8,128)S(1)}, f32[1,2,2048,256]{3,2,1,0:T(8,128)}, u32[]{:S(2)}) copy-start(f32[1,2,2048,256]{3,2,1,0:T(8,128)} %param.3) | copy-start | bytes 12582916
  76.4 8.9 %collective-permute-start.1 = (f32[1,2,64,256]{3,2,1,0:T(8,128)S(1)}, f32[1,2,64,256]{3,2,1,0:T(8,128)S(1)}, u32[]{:S(2)}, u32[]{:S(2)}) collective-permute-start(f32[1,2,64,256]{3,2,1,0:T(8,128)S(1)} %add.33), channel_id=1, source_target_pairs={{0,8},{8,16},{16,24},{24,32},{32,40},{40,48},{48,56},{56,64},{64,7... | collective-permute-start | bytes 393224 | tf_op jit(solution)/shard_map/ppermute | solution.py:12
  97.9 104.3 %reduce-scatter.9.cloned.1.call-start = ((), (), s32[]{:S(2)}) async-start(), calls=%async_computation.6 | async-start | bytes 1179648 | tf_op jit(solution)/shard_map/reduce_scatter | solution.py:42
  138.7 17.3 %copy-start.2 = (f32[1,2,2048,256]{3,2,1,0:T(8,128)S(1)}, f32[1,2,2048,256]{3,2,1,0:T(8,128)}, u32[]{:S(2)}) copy-start(f32[1,2,2048,256]{3,2,1,0:T(8,128)} %param.3) | copy-start | bytes 12582916
  139.8 8.9 %collective-permute-start.2 = (f32[1,2,64,256]{3,2,1,0:T(8,128)S(1)}, f32[1,2,64,256]{3,2,1,0:T(8,128)S(1)}, u32[]{:S(2)}, u32[]{:S(2)}) collective-permute-start(f32[1,2,64,256]{3,2,1,0:T(8,128)S(1)} %add.35), channel_id=1, source_target_pairs={{0,8},{8,16},{16,24},{24,32},{32,40},{40,48},{48,56},{56,64},{64,7... | collective-permute-start | bytes 393224 | tf_op jit(solution)/shard_map/ppermute | solution.py:12
  161.3 104.3 %reduce-scatter.11.cloned.1.call-start = ((), (), s32[]{:S(2)}) async-start(), calls=%async_computation.7 | async-start | bytes 1179648 | tf_op jit(solution)/shard_map/reduce_scatter | solution.py:42
  202.2 17.3 %copy-start.3 = (f32[1,2,2048,256]{3,2,1,0:T(8,128)S(1)}, f32[1,2,2048,256]{3,2,1,0:T(8,128)}, u32[]{:S(2)}) copy-start(f32[1,2,2048,256]{3,2,1,0:T(8,128)} %param.3) | copy-start | bytes 12582916
  203.3 8.9 %collective-permute-start.3 = (f32[1,2,64,256]{3,2,1,0:T(8,128)S(1)}, f32[1,2,64,256]{3,2,1,0:T(8,128)S(1)}, u32[]{:S(2)}, u32[]{:S(2)}) collective-permute-start(f32[1,2,64,256]{3,2,1,0:T(8,128)S(1)} %add.37), channel_id=1, source_target_pairs={{0,8},{8,16},{16,24},{24,32},{32,40},{40,48},{48,56},{56,64},{64,7... | collective-permute-start | bytes 393224 | tf_op jit(solution)/shard_map/ppermute | solution.py:12
Sparse Core Ops, SparseCore 0:
  30.2 45.0 reduce-scatter.4
  98.0 40.6 reduce-scatter.6
  161.5 40.7 reduce-scatter.8
  225.0 40.5 reduce-scatter.10
where the time goes:
time: 276 us; the launch traced here: 274 us
  waiting for transfers between devices  194 us (70%)
  matrix products  46.5 us (17%)
  between operations  13.2 us (5%)
  starting transfers between devices  11.3 us (4%)
  other arithmetic  8.94 us (3%)
    reduce_scatter x4, waiting for transfers between devices, shards(): lax.psum_scatter(partial_value, 'col', scatter_dimension=3, tiled=True)  168 us
    dot_general x16, matrix products, matmul_t(): lax.dot_general(left, right, (((1,), (1,)), ((), ())), precision=lax.Prec...  46.5 us
    ppermute x4, waiting for transfers between devices, from_behind(): return lax.ppermute(block, axis, route)  26.2 us
    ppermute x4, starting transfers between devices, from_behind(): return lax.ppermute(block, axis, route)  11.2 us
  transfers between devices with their start and end apart: 8, of which 8 were waited for; matrix products, arithmetic and copies ran while one was open for 0% of the time, Pallas kernels for 0%

commit v1 on v0

v1 whole, which is shorter than its diff:
```python
import jax
import jax.numpy as jnp
from jax import lax
from jax.experimental import pallas as pl
from jax.experimental.pallas import tpu as pltpu
from jax.sharding import PartitionSpec as P

STEPS = 4
GROUPS = 2
CHIPS = 4
MESH = pl.DeviceIdType.MESH
F32 = jnp.float32
BF16 = jnp.bfloat16

FAR_A, FAR_B, NEAR_A, NEAR_B = range(4)
LAST_FAR_A, LAST_FAR_B, LAST_DIRECT_A, LAST_DIRECT_B, LAST_SUM_A, LAST_SUM_B = range(6)


def pack(block, group):
    shots = pl.ds(32 * group, 32)
    rows = [block[part, shots, pl.ds(128 * half, 128)] for half in range(2) for part in range(2)]
    return jnp.concatenate(rows, 0).T


def split(value):
    high = value.astype(BF16)
    return high, (value - high.astype(F32)).astype(BF16)


def kernel(
    green, traces, sources, swept,
    staged, left, right, source_block, incoming, held, partner_held,
    far_out, far_in, near_own, near_out, near_in, last_own, last_out, last_in,
    green_local_sem, green_send_sem, green_recv_sem, source_sem, first_send_sem, first_recv_sem,
    share_send_sem, share_recv_sem, far_send_sem, far_recv_sem, near_send_sem, near_recv_sem,
    last_send_sem, last_recv_sem,
):
    slabs = lax.axis_size("slab")
    slab, col = lax.axis_index("slab"), lax.axis_index("col")
    chip, core = col // 2, col % 2
    sigma = 1 - 2 * (slab % 2)
    below, above = (slab + 1) % slabs, (slab + slabs - 1) % slabs
    ahead, behind, across = (chip + sigma + CHIPS) % CHIPS, (chip - sigma + CHIPS) % CHIPS, (chip + 2) % CHIPS
    at = lambda s, c, k=core: (s, 2 * c + k)
    partner = at(slab, chip, 1 - core)
    sent = []

    def send(source, target, send_sem, recv_sem, device):
        copy = pltpu.make_async_remote_copy(
            src_ref=source, dst_ref=target, send_sem=send_sem, recv_sem=recv_sem, device_id=device, device_id_type=MESH
        )
        copy.start()
        sent.append(copy)

    def arrived(target, recv_sem):
        pltpu.make_async_copy(target, target, recv_sem).wait()

    barrier = pltpu.get_barrier_semaphore()
    senders = (at(slab, ahead), at(slab, behind), partner, at(above, chip), at(above, behind))
    for device in senders:
        pl.semaphore_signal(barrier, inc=1, device_id=device, device_id_type=MESH)

    slot_chips = (ahead, across, chip, behind)

    def green_rows(slot, k):
        return green.at[0, :, pl.ds(pl.multiple_of(512 * slot_chips[slot] + 256 * k, 256), 256), :]

    local = []
    for slot in range(CHIPS):
        copy = pltpu.make_async_copy(green_rows(slot, core), staged.at[0, slot], green_local_sem.at[slot])
        copy.start()
        local.append(copy)
    source_copy = pltpu.make_async_copy(sources.at[0], source_block, source_sem)
    source_copy.start()

    pl.semaphore_wait(barrier, len(senders))
    for group in range(GROUPS):
        send(
            traces.at[0, :, pl.ds(32 * group, 32), :], incoming.at[group],
            first_send_sem.at[group], first_recv_sem.at[group], at(below, chip),
        )
    for slot in range(CHIPS):
        send(
            green_rows(slot, 1 - core), staged.at[1, slot], green_send_sem.at[slot], green_recv_sem.at[slot], partner
        )

    def convert(origin, slot):
        for part in range(2):
            for half in range(2):
                high, low = split(staged[origin, slot, part, pl.ds(128 * half, 128), :])
                columns = pl.ds(256 * ((part * 2 + origin) * 2 + half), 256)
                left[slot, pl.ds(0, 128), columns] = high
                left[slot, pl.ds(128, 128), columns] = low

    for slot in range(CHIPS):
        local[slot].wait()
        convert(0, slot)
    source_copy.wait()

    def share(step, group, value):
        value = jnp.where(slab == 0, jnp.zeros_like(value), value)
        held[step, group] = value
        send(
            held.at[step, group], partner_held.at[step, group],
            share_send_sem.at[step, group], share_recv_sem.at[step, group], partner,
        )

    lane = lax.broadcasted_iota(jnp.int32, (128, 128), 1)
    low_lanes = lane < 64
    real_lanes = lane % 64 < 32

    def make_right(step, group):
        arrived(partner_held.at[step, group], share_recv_sem.at[step, group])
        for origin in range(2):
            value = (held if origin == 0 else partner_held)[step, group]
            turned = jnp.where(real_lanes, -pltpu.roll(value, 96, 1), pltpu.roll(value, 32, 1))
            for part, term in ((0, value), (1, turned)):
                swapped = pltpu.roll(term, 64, 1)
                quarters = (
                    jnp.where(low_lanes, term, 0.0), jnp.where(low_lanes, swapped, 0.0),
                    jnp.where(low_lanes, 0.0, swapped), jnp.where(low_lanes, 0.0, term),
                )
                for index, quarter in enumerate(quarters):
                    high, low = split(quarter)
                    rows = pl.ds(256 * ((part * 2 + origin) * 2) + 128 * index, 128)
                    right[group, rows, pl.ds(0, 128)] = high
                    right[group, rows, pl.ds(128, 128)] = low

    def product(group, slot):
        full = jnp.dot(left[slot], right[group], preferred_element_type=F32)
        return (full[:128, :128] + full[:128, 128:]) + (full[128:, :128] + full[128:, 128:])

    def send_far(step, group):
        for slot, device in ((FAR_A, at(slab, ahead)), (FAR_B, at(slab, behind))):
            far_out[step, group, slot] = product(group, slot)
            send(
                far_out.at[step, group, slot], far_in.at[step, group, slot],
                far_send_sem.at[step, group, slot], far_recv_sem.at[step, group, slot], device,
            )

    def own_near(step, group):
        near_own[group, 0] = product(group, NEAR_A) + pack(source_block, group)
        near_own[group, 1] = product(group, NEAR_B)

    def send_near(step, group):
        for side, device in ((0, at(below, chip)), (1, at(below, behind))):
            arrived(far_in.at[step, group, side], far_recv_sem.at[step, group, side])
            near_out[step, group, side] = near_own[group, side] + far_in[step, group, side]
            send(
                near_out.at[step, group, side], near_in.at[step, group, side],
                near_send_sem.at[step, group, side], near_recv_sem.at[step, group, side], device,
            )

    def take_near(step, group):
        for side in range(2):
            arrived(near_in.at[step, group, side], near_recv_sem.at[step, group, side])
        share(step + 1, group, near_in[step, group, 0] + near_in[step, group, 1])

    def send_last(group, which, device):
        send(
            last_out.at[group, which], last_in.at[group, which],
            last_send_sem.at[group, which], last_recv_sem.at[group, which], device,
        )

    def last_products(group):
        forward, backward = at(slab, ahead), at(slab, behind)
        far = product(group, FAR_B)
        last_out[group, LAST_FAR_A] = far[:64]
        send_last(group, LAST_FAR_A, forward)
        last_out[group, LAST_FAR_B] = far[64:]
        send_last(group, LAST_FAR_B, backward)
        near = product(group, FAR_A)
        last_out[group, LAST_DIRECT_A] = near[64:]
        send_last(group, LAST_DIRECT_A, forward)
        last_own[group, pl.ds(0, 64)] = near[:64]
        near = product(group, NEAR_B)
        last_out[group, LAST_DIRECT_B] = near[:64]
        send_last(group, LAST_DIRECT_B, backward)
        last_own[group, pl.ds(64, 64)] = near[64:]
        near_own[group, 0] = product(group, NEAR_A) + pack(source_block, group)

    def last_relay(group):
        for side, device in ((0, at(slab, ahead)), (1, at(slab, behind))):
            far, out = LAST_FAR_A + side, LAST_SUM_A + side
            arrived(last_in.at[group, far], last_recv_sem.at[group, far])
            last_out[group, out] = last_own[group, pl.ds(64 * side, 64)] + last_in[group, far]
            send_last(group, out, device)

    def last_take(group):
        for which in (LAST_DIRECT_A, LAST_DIRECT_B, LAST_SUM_A, LAST_SUM_B):
            arrived(last_in.at[group, which], last_recv_sem.at[group, which])
        top = near_own[group, 0, pl.ds(0, 64)] + (last_in[group, LAST_SUM_A] + last_in[group, LAST_DIRECT_B])
        bottom = near_own[group, 0, pl.ds(64, 64)] + (last_in[group, LAST_SUM_B] + last_in[group, LAST_DIRECT_A])
        rows = jnp.concatenate([top, bottom], 0).T
        for half in range(2):
            for part in range(2):
                swept[0, part, pl.ds(32 * group, 32), pl.ds(128 * half, 128)] = rows[32 * (2 * half + part) :][:32]

    for group in range(GROUPS):
        arrived(incoming.at[group], first_recv_sem.at[group])
        share(0, group, pack(incoming.at[group], 0))
    for slot in range(CHIPS):
        arrived(staged.at[1, slot], green_recv_sem.at[slot])
        convert(1, slot)
    for group in range(GROUPS):
        make_right(0, group)
        send_far(0, group)
        own_near(0, group)
    for step in range(STEPS - 1):
        for group in range(GROUPS):
            send_near(step, group)
        for group in range(GROUPS):
            take_near(step, group)
            make_right(step + 1, group)
            if step + 1 < STEPS - 1:
                send_far(step + 1, group)
                own_near(step + 1, group)
            else:
                last_products(group)
    for group in range(GROUPS):
        last_relay(group)
    for group in range(GROUPS):
        last_take(group)
    for copy in sent:
        copy.wait_send()


def sweep(green_blocks, traces, sources):
    steps, dma = STEPS - 1, pltpu.SemaphoreType.DMA
    return pl.pallas_call(
        kernel,
        out_shape=jax.ShapeDtypeStruct(traces.shape, F32),
        in_specs=[pl.BlockSpec(memory_space=pl.ANY)] * 3,
        out_specs=pl.BlockSpec(memory_space=pltpu.VMEM),
        scratch_shapes=[
            pltpu.VMEM((2, CHIPS, 2, 256, 256), F32),
            pltpu.VMEM((CHIPS, 256, 2048), BF16),
            pltpu.VMEM((GROUPS, 2048, 256), BF16),
            pltpu.VMEM((2, 64, 256), F32),
            pltpu.VMEM((GROUPS, 2, 32, 256), F32),
            pltpu.VMEM((STEPS, GROUPS, 128, 128), F32),
            pltpu.VMEM((STEPS, GROUPS, 128, 128), F32),
            pltpu.VMEM((steps, GROUPS, 2, 128, 128), F32),
            pltpu.VMEM((steps, GROUPS, 2, 128, 128), F32),
            pltpu.VMEM((GROUPS, 2, 128, 128), F32),
            pltpu.VMEM((steps, GROUPS, 2, 128, 128), F32),
            pltpu.VMEM((steps, GROUPS, 2, 128, 128), F32),
            pltpu.VMEM((GROUPS, 128, 128), F32),
            pltpu.VMEM((GROUPS, 6, 64, 128), F32),
            pltpu.VMEM((GROUPS, 6, 64, 128), F32),
            dma((CHIPS,)), dma((CHIPS,)), dma((CHIPS,)), dma, dma((GROUPS,)), dma((GROUPS,)),
            dma((STEPS, GROUPS)), dma((STEPS, GROUPS)),
            dma((steps, GROUPS, 2)), dma((steps, GROUPS, 2)), dma((steps, GROUPS, 2)), dma((steps, GROUPS, 2)),
            dma((GROUPS, 6)), dma((GROUPS, 6)),
        ],
        compiler_params=pltpu.CompilerParams(
            collective_id=0, has_side_effects=True, vmem_limit_bytes=48 * 1024 * 1024
        ),
        name="sweep",
    )(green_blocks, traces, sources)


def solution(mesh):
    placed = P("slab", None, None, "col")
    return jax.shard_map(sweep, mesh=mesh, in_specs=(placed,) * 3, out_specs=placed, check_vma=False)
```

time: 276 us -> 78.9 us (0.29)
  the two profiles are of different devices: /device:TPU:7 before, /device:TPU:9 now
where the time goes in v1:
time: 78.9 us; the launch traced here: 78.7 us
  Pallas kernels  74 us (94%)
  local copies, waits for them, and re-layouts  4.65 us (6%)
    pallas_call x1, Pallas kernels, sweep(): pl.pallas_call(kernel, out_shape=jax.ShapeDtypeStruct(traces.shape, F32),...  74 us
    unnamed x7, local copies, waits for them, and re-layouts  4.65 us

profile of v1, /device:TPU:9, one launch (start us, length us, event | category | flops | bytes accessed | tf_op | source)
XLA Modules:
  0.0 78.7 jit_solution(18280765680479098448)
XLA Ops:
  0.0 0.0 copy-start
  0.0 2.2 %copy-done = f32[1,2,2048,256]{3,2,1,0:T(8,128)S(1)} copy-done((f32[1,2,2048,256]{3,2,1,0:T(8,128)S(1)}, f32[1,2,2048,256]{3,2,1,0:T(8,128)}, u32[]{:S(2)}) %copy-start) | copy-done | bytes 4194328
  2.2 0.0 copy-start.1
  2.2 0.9 %copy-done.1 = f32[1,2,64,256]{3,2,1,0:T(8,128)S(1)} copy-done((f32[1,2,64,256]{3,2,1,0:T(8,128)S(1)}, f32[1,2,64,256]{3,2,1,0:T(8,128)}, u32[]{:S(2)}) %copy-start.1) | copy-done | bytes 131096
  3.1 0.0 copy-start.2
  3.1 0.9 %copy-done.2 = f32[1,2,64,256]{3,2,1,0:T(8,128)S(1)} copy-done((f32[1,2,64,256]{3,2,1,0:T(8,128)S(1)}, f32[1,2,64,256]{3,2,1,0:T(8,128)}, u32[]{:S(2)}) %copy-start.2) | copy-done | bytes 131096
  4.0 74.0 %sweep.1 = f32[1,2,64,256]{3,2,1,0:T(8,128)S(1)} custom-call(f32[1,2,2048,256]{3,2,1,0:T(8,128)S(1)} %copy-done, f32[1,2,64,256]{3,2,1,0:T(8,128)S(1)} %copy-done.1, f32[1,2,64,256]{3,2,1,0:T(8,128)S(1)} %copy-done.2), custom_call_target="tpu_custom_call" | custom-call | tf_op jit(solution)/shard_map/sweep/pallas_call | solution.py:230
  78.0 0.7 copy.5
Async XLA Ops:
  0.0 2.2 %copy-start = (f32[1,2,2048,256]{3,2,1,0:T(8,128)S(1)}, f32[1,2,2048,256]{3,2,1,0:T(8,128)}, u32[]{:S(2)}) copy-start(f32[1,2,2048,256]{3,2,1,0:T(8,128)} %green.1) | copy-start | bytes 12582916
  2.2 0.9 %copy-start.1 = (f32[1,2,64,256]{3,2,1,0:T(8,128)S(1)}, f32[1,2,64,256]{3,2,1,0:T(8,128)}, u32[]{:S(2)}) copy-start(f32[1,2,64,256]{3,2,1,0:T(8,128)} %traces.1) | copy-start | bytes 393220
  3.1 0.9 %copy-start.2 = (f32[1,2,64,256]{3,2,1,0:T(8,128)S(1)}, f32[1,2,64,256]{3,2,1,0:T(8,128)}, u32[]{:S(2)}) copy-start(f32[1,2,64,256]{3,2,1,0:T(8,128)} %sources.1) | copy-start | bytes 393220

commit v2 on v1

v2 whole, which is shorter than its diff:
```python
import jax
import jax.numpy as jnp
from jax import lax
from jax.experimental import pallas as pl
from jax.experimental.pallas import tpu as pltpu
from jax.sharding import PartitionSpec as P

STEPS = 4
GROUPS = 2
CHIPS = 4
PIECES = 2
PIECE = 128 // PIECES
MESH = pl.DeviceIdType.MESH
F32 = jnp.float32
BF16 = jnp.bfloat16

FAR_A, FAR_B, NEAR_A, NEAR_B = range(4)
LAST_FAR_A, LAST_FAR_B, LAST_DIRECT_A, LAST_DIRECT_B, LAST_SUM_A, LAST_SUM_B = range(6)


def pack(block, group):
    shots = pl.ds(32 * group, 32)
    rows = [block[part, shots, pl.ds(128 * half, 128)] for half in range(2) for part in range(2)]
    return jnp.concatenate(rows, 0).T


def split(value):
    high = value.astype(BF16)
    return high, (value - high.astype(F32)).astype(BF16)


def kernel(
    green, traces, sources, swept,
    staged, left, right, source_block, incoming, held, partner_held,
    begun, far_out, far_in, near_own, near_out, near_in, last_own, last_out, last_in, last_near_out, last_near_in,
    green_local_sem, green_send_sem, green_recv_sem, source_send_sem, source_recv_sem, first_send_sem, first_recv_sem,
    share_send_sem, share_recv_sem, far_send_sem, far_recv_sem, near_send_sem, near_recv_sem,
    last_send_sem, last_recv_sem, last_near_send_sem, last_near_recv_sem,
):
    slabs = lax.axis_size("slab")
    slab, col = lax.axis_index("slab"), lax.axis_index("col")
    chip, core = col // 2, col % 2
    sigma = 1 - 2 * (slab % 2)
    below, above = (slab + 1) % slabs, (slab + slabs - 1) % slabs
    ahead, behind, across = (chip + sigma + CHIPS) % CHIPS, (chip - sigma + CHIPS) % CHIPS, (chip + 2) % CHIPS
    at = lambda s, c, k=core: (s, 2 * c + k)
    partner = at(slab, chip, 1 - core)
    sent = []

    def send(source, target, send_sem, recv_sem, device):
        copy = pltpu.make_async_remote_copy(
            src_ref=source, dst_ref=target, send_sem=send_sem, recv_sem=recv_sem, device_id=device, device_id_type=MESH
        )
        copy.start()
        sent.append(copy)

    def arrived(target, recv_sem):
        pltpu.make_async_copy(target, target, recv_sem).wait()

    barrier = pltpu.get_barrier_semaphore()
    other = 1 - core
    senders = (
        at(slab, behind), at(slab, behind, other), at(slab, ahead, other), partner,
        at(above, chip), at(above, chip, other), at(above, behind, other),
    )
    for device in senders:
        pl.semaphore_signal(barrier, inc=1, device_id=device, device_id_type=MESH)

    slot_chips = (ahead, across, chip, behind)

    def green_rows(slot, k):
        owner = k if slot in (FAR_A, FAR_B) else 1 - k
        return green.at[0, :, pl.ds(pl.multiple_of(512 * slot_chips[slot] + 256 * owner, 256), 256), :]

    local = []
    for slot in range(CHIPS):
        copy = pltpu.make_async_copy(green_rows(slot, core), staged.at[0, slot], green_local_sem.at[slot])
        copy.start()
        local.append(copy)

    pl.semaphore_wait(barrier, len(senders))
    for group in range(GROUPS):
        send(
            traces.at[0, :, pl.ds(32 * group, 32), :], incoming.at[group],
            first_send_sem.at[group], first_recv_sem.at[group], at(below, chip),
        )
    for slot in range(CHIPS):
        send(
            green_rows(slot, 1 - core), staged.at[1, slot], green_send_sem.at[slot], green_recv_sem.at[slot], partner
        )
    send(sources.at[0], source_block, source_send_sem, source_recv_sem, partner)

    def convert(origin, slot):
        for part in range(2):
            for half in range(2):
                high, low = split(staged[origin, slot, part, pl.ds(128 * half, 128), :])
                columns = pl.ds(256 * ((origin * 2 + part) * 2 + half), 256)
                left[slot, pl.ds(0, 128), columns] = high
                left[slot, pl.ds(128, 128), columns] = low

    for slot in range(CHIPS):
        local[slot].wait()
        convert(0, slot)
    for slot in range(CHIPS):
        arrived(staged.at[1, slot], green_recv_sem.at[slot])
        convert(1, slot)
    arrived(source_block, source_recv_sem)

    def share(step, group, value):
        value = jnp.where(slab == 0, jnp.zeros_like(value), value)
        held[step, group] = value
        send(
            held.at[step, group], partner_held.at[step, group],
            share_send_sem.at[step, group], share_recv_sem.at[step, group], partner,
        )

    lane = lax.broadcasted_iota(jnp.int32, (128, 128), 1)
    low_lanes = lane < 64
    real_lanes = lane % 64 < 32

    def make_right(step, group, origin):
        value = (held if origin == 0 else partner_held)[step, group]
        turned = jnp.where(real_lanes, -pltpu.roll(value, 96, 1), pltpu.roll(value, 32, 1))
        for part, term in ((0, value), (1, turned)):
            swapped = pltpu.roll(term, 64, 1)
            quarters = (
                jnp.where(low_lanes, term, 0.0), jnp.where(low_lanes, swapped, 0.0),
                jnp.where(low_lanes, 0.0, swapped), jnp.where(low_lanes, 0.0, term),
            )
            for index, quarter in enumerate(quarters):
                high, low = split(quarter)
                rows = pl.ds(256 * ((origin * 2 + part) * 2) + 128 * index, 128)
                right[group, rows, pl.ds(0, 128)] = high
                right[group, rows, pl.ds(128, 128)] = low

    def product(group, slot, depth=slice(None)):
        full = jnp.dot(left[slot, :, depth], right[group, depth, :], preferred_element_type=F32)
        return (full[:128, :128] + full[:128, 128:]) + (full[128:, :128] + full[128:, 128:])

    def begin(step, group):
        make_right(step, group, 0)
        for slot in (FAR_A, FAR_B) if step < STEPS - 1 else (FAR_B,):
            begun[group, slot] = product(group, slot, slice(0, 1024))

    def send_far(step, group):
        arrived(partner_held.at[step, group], share_recv_sem.at[step, group])
        make_right(step, group, 1)
        if step == STEPS - 1:
            last_products(group)
            return
        for slot, device in ((FAR_A, at(slab, ahead, other)), (FAR_B, at(slab, behind, other))):
            far_out[step, group, slot] = begun[group, slot] + product(group, slot, slice(1024, 2048))
            for piece in range(PIECES):
                rows = pl.ds(PIECE * piece, PIECE)
                send(
                    far_out.at[step, group, slot, rows], far_in.at[step, group, slot, rows],
                    far_send_sem.at[step, group, slot, piece], far_recv_sem.at[step, group, slot, piece], device,
                )

    def near_products(step, group):
        if step == STEPS - 1:
            last_near_products(group)
            return
        near_own[group, 0] = product(group, NEAR_A) + pack(source_block, group)
        near_own[group, 1] = product(group, NEAR_B)

    def send_near(step, group):
        for piece in range(PIECES):
            rows = pl.ds(PIECE * piece, PIECE)
            for side, device in ((0, at(below, chip, other)), (1, at(below, behind, other))):
                arrived(far_in.at[step, group, side, rows], far_recv_sem.at[step, group, side, piece])
                near_out[step, group, side, rows] = near_own[group, side, rows] + far_in[step, group, side, rows]
                send(
                    near_out.at[step, group, side, rows], near_in.at[step, group, side, rows],
                    near_send_sem.at[step, group, side, piece], near_recv_sem.at[step, group, side, piece], device,
                )

    def take_near(step, group):
        for piece in range(PIECES):
            for side in range(2):
                rows = pl.ds(PIECE * piece, PIECE)
                arrived(near_in.at[step, group, side, rows], near_recv_sem.at[step, group, side, piece])
        share(step + 1, group, near_in[step, group, 0] + near_in[step, group, 1])

    def send_last(group, which, device):
        send(
            last_out.at[group, which], last_in.at[group, which],
            last_send_sem.at[group, which], last_recv_sem.at[group, which], device,
        )

    def last_products(group):
        forward, backward = at(slab, ahead), at(slab, behind, other)
        far = begun[group, FAR_B] + product(group, FAR_B, slice(1024, 2048))
        last_out[group, LAST_FAR_A] = far[:64]
        send_last(group, LAST_FAR_A, forward)
        last_out[group, LAST_FAR_B] = far[64:]
        send_last(group, LAST_FAR_B, backward)
        near = product(group, FAR_A)
        last_out[group, LAST_DIRECT_A] = near[64:]
        send_last(group, LAST_DIRECT_A, forward)
        last_own[group, pl.ds(0, 64)] = near[:64]
        near = product(group, NEAR_B)
        last_out[group, LAST_DIRECT_B] = near[:64]
        send_last(group, LAST_DIRECT_B, backward)
        last_own[group, pl.ds(64, 64)] = near[64:]

    def last_near_products(group):
        last_near_out[group] = product(group, NEAR_A) + pack(source_block, group)
        send(
            last_near_out.at[group], last_near_in.at[group],
            last_near_send_sem.at[group], last_near_recv_sem.at[group], partner,
        )

    def last_relay(group):
        for side, device in ((0, at(slab, ahead)), (1, at(slab, behind, other))):
            far, out = LAST_FAR_A + side, LAST_SUM_A + side
            arrived(last_in.at[group, far], last_recv_sem.at[group, far])
            last_out[group, out] = last_own[group, pl.ds(64 * side, 64)] + last_in[group, far]
            send_last(group, out, device)

    def last_take(group):
        arrived(last_near_in.at[group], last_near_recv_sem.at[group])
        for which in (LAST_DIRECT_A, LAST_DIRECT_B, LAST_SUM_A, LAST_SUM_B):
            arrived(last_in.at[group, which], last_recv_sem.at[group, which])
        top = last_near_in[group, pl.ds(0, 64)] + (last_in[group, LAST_SUM_A] + last_in[group, LAST_DIRECT_B])
        bottom = last_near_in[group, pl.ds(64, 64)] + (last_in[group, LAST_SUM_B] + last_in[group, LAST_DIRECT_A])
        rows = jnp.concatenate([top, bottom], 0).T
        for half in range(2):
            for part in range(2):
                swept[0, part, pl.ds(32 * group, 32), pl.ds(128 * half, 128)] = rows[32 * (2 * half + part) :][:32]

    def relay(step, group):
        last_relay(group) if step == STEPS - 1 else send_near(step, group)

    def take(step, group):
        last_take(group) if step == STEPS - 1 else take_near(step, group)

    for group in range(GROUPS):
        arrived(incoming.at[group], first_recv_sem.at[group])
        share(0, group, pack(incoming.at[group], 0))
        begin(0, group)
    send_far(0, 0)
    send_far(0, 1)
    for step in range(STEPS):
        for group in range(GROUPS):
            near_products(step, group)
        for group in range(GROUPS):
            relay(step, group)
        for group in range(GROUPS):
            take(step, group)
            if step + 1 < STEPS:
                begin(step + 1, group)
                send_far(step + 1, group)
    for copy in sent:
        copy.wait_send()


def sweep(green_blocks, traces, sources):
    steps, dma = STEPS - 1, pltpu.SemaphoreType.DMA
    return pl.pallas_call(
        kernel,
        out_shape=jax.ShapeDtypeStruct(traces.shape, F32),
        in_specs=[pl.BlockSpec(memory_space=pltpu.HBM)] * 3,
        out_specs=pl.BlockSpec(memory_space=pltpu.VMEM),
        scratch_shapes=[
            pltpu.VMEM((2, CHIPS, 2, 256, 256), F32),
            pltpu.VMEM((CHIPS, 256, 2048), BF16),
            pltpu.VMEM((GROUPS, 2048, 256), BF16),
            pltpu.VMEM((2, 64, 256), F32),
            pltpu.VMEM((GROUPS, 2, 32, 256), F32),
            pltpu.VMEM((STEPS, GROUPS, 128, 128), F32),
            pltpu.VMEM((STEPS, GROUPS, 128, 128), F32),
            pltpu.VMEM((GROUPS, 2, 128, 128), F32),
            pltpu.VMEM((steps, GROUPS, 2, 128, 128), F32),
            pltpu.VMEM((steps, GROUPS, 2, 128, 128), F32),
            pltpu.VMEM((GROUPS, 2, 128, 128), F32),
            pltpu.VMEM((steps, GROUPS, 2, 128, 128), F32),
            pltpu.VMEM((steps, GROUPS, 2, 128, 128), F32),
            pltpu.VMEM((GROUPS, 128, 128), F32),
            pltpu.VMEM((GROUPS, 6, 64, 128), F32),
            pltpu.VMEM((GROUPS, 6, 64, 128), F32),
            pltpu.VMEM((GROUPS, 128, 128), F32),
            pltpu.VMEM((GROUPS, 128, 128), F32),
            dma((CHIPS,)), dma((CHIPS,)), dma((CHIPS,)), dma, dma, dma((GROUPS,)), dma((GROUPS,)),
            dma((STEPS, GROUPS)), dma((STEPS, GROUPS)),
            dma((steps, GROUPS, 2, PIECES)), dma((steps, GROUPS, 2, PIECES)),
            dma((steps, GROUPS, 2, PIECES)), dma((steps, GROUPS, 2, PIECES)),
            dma((GROUPS, 6)), dma((GROUPS, 6)), dma((GROUPS,)), dma((GROUPS,)),
        ],
        compiler_params=pltpu.CompilerParams(
            collective_id=0, has_side_effects=True, vmem_limit_bytes=67043328
        ),
        name="sweep",
    )(green_blocks, traces, sources)


def solution(mesh):
    placed = P("slab", None, None, "col")
    return jax.shard_map(sweep, mesh=mesh, in_specs=(placed,) * 3, out_specs=placed, check_vma=False)
```

time: 78.9 us -> 74.5 us (0.944)
  the two profiles are of different devices: /device:TPU:9 before, /device:TPU:1 now
where the time goes in v2:
time: 74.5 us; the launch traced here: 74.4 us
  Pallas kernels  72.8 us (98%)
  local copies, waits for them, and re-layouts  1.57 us (2%)
    pallas_call x1, Pallas kernels, sweep(): pl.pallas_call(kernel, out_shape=jax.ShapeDtypeStruct(traces.shape, F32),...  72.8 us
    unnamed x1, local copies, waits for them, and re-layouts  1.57 us

profile of v2, /device:TPU:1, one launch (start us, length us, event | category | flops | bytes accessed | tf_op | source)
XLA Modules:
  0.0 74.4 jit_solution(2647024701372389707)
XLA Ops:
  0.0 72.8 %sweep.1 = f32[1,2,64,256]{3,2,1,0:T(8,128)} custom-call(f32[1,2,2048,256]{3,2,1,0:T(8,128)} %green.1, f32[1,2,64,256]{3,2,1,0:T(8,128)} %traces.1, f32[1,2,64,256]{3,2,1,0:T(8,128)} %sources.1), custom_call_target="tpu_custom_call" | custom-call | tf_op jit(solution)/shard_map/sweep/pallas_call | solution.py:260
  72.8 1.6 %copy.5 = f32[1,2,64,256]{3,2,1,0:T(8,128)} copy(f32[1,2,64,256]{3,2,1,0:T(8,128)} %sweep.1) | data formatting | bytes 262144

commit v3 on v2

--- a/solution.py
+++ b/solution.py
@@ -45,7 +45,7 @@
     ahead, behind, across = (chip + sigma + CHIPS) % CHIPS, (chip - sigma + CHIPS) % CHIPS, (chip + 2) % CHIPS
     at = lambda s, c, k=core: (s, 2 * c + k)
     partner = at(slab, chip, 1 - core)
-    sent = []
+    sent, sent_below = [], []
 
     def send(source, target, send_sem, recv_sem, device):
         copy = pltpu.make_async_remote_copy(
@@ -54,17 +54,29 @@
         copy.start()
         sent.append(copy)
 
+    is_first, is_last = slab == 0, slab == slabs - 1
+
+    def send_below(source, target, send_sem, recv_sem, device):
+        copy = pltpu.make_async_remote_copy(
+            src_ref=source, dst_ref=target, send_sem=send_sem, recv_sem=recv_sem, device_id=device, device_id_type=MESH
+        )
+        pl.when(jnp.logical_not(is_last))(copy.start)
+        sent_below.append(copy)
+
     def arrived(target, recv_sem):
         pltpu.make_async_copy(target, target, recv_sem).wait()
 
     barrier = pltpu.get_barrier_semaphore()
     other = 1 - core
-    senders = (
-        at(slab, behind), at(slab, behind, other), at(slab, ahead, other), partner,
-        at(above, chip), at(above, chip, other), at(above, behind, other),
-    )
-    for device in senders:
+    same_slab = (at(slab, behind), at(slab, behind, other), at(slab, ahead, other), partner)
+    from_above = (at(above, chip), at(above, chip, other), at(above, behind, other))
+    for device in same_slab:
         pl.semaphore_signal(barrier, inc=1, device_id=device, device_id_type=MESH)
+
+    @pl.when(jnp.logical_not(is_first))
+    def _():
+        for device in from_above:
+            pl.semaphore_signal(barrier, inc=1, device_id=device, device_id_type=MESH)
 
     slot_chips = (ahead, across, chip, behind)
 
@@ -78,9 +90,16 @@
         copy.start()
         local.append(copy)
 
-    pl.semaphore_wait(barrier, len(senders))
+    @pl.when(is_last)
+    def _():
+        pl.semaphore_wait(barrier, len(same_slab))
+
+    @pl.when(jnp.logical_not(is_last))
+    def _():
+        pl.semaphore_wait(barrier, len(same_slab) + len(from_above))
+
     for group in range(GROUPS):
-        send(
+        send_below(
             traces.at[0, :, pl.ds(32 * group, 32), :], incoming.at[group],
             first_send_sem.at[group], first_recv_sem.at[group], at(below, chip),
         )
@@ -106,9 +125,15 @@
         convert(1, slot)
     arrived(source_block, source_recv_sem)
 
-    def share(step, group, value):
-        value = jnp.where(slab == 0, jnp.zeros_like(value), value)
-        held[step, group] = value
+    def share(step, group, value_of):
+        @pl.when(is_first)
+        def _():
+            held[step, group] = jnp.zeros((128, 128), F32)
+
+        @pl.when(jnp.logical_not(is_first))
+        def _():
+            held[step, group] = value_of()
+
         send(
             held.at[step, group], partner_held.at[step, group],
             share_send_sem.at[step, group], share_recv_sem.at[step, group], partner,
@@ -170,17 +195,27 @@
             for side, device in ((0, at(below, chip, other)), (1, at(below, behind, other))):
                 arrived(far_in.at[step, group, side, rows], far_recv_sem.at[step, group, side, piece])
                 near_out[step, group, side, rows] = near_own[group, side, rows] + far_in[step, group, side, rows]
-                send(
+                send_below(
                     near_out.at[step, group, side, rows], near_in.at[step, group, side, rows],
                     near_send_sem.at[step, group, side, piece], near_recv_sem.at[step, group, side, piece], device,
                 )
 
     def take_near(step, group):
-        for piece in range(PIECES):
-            for side in range(2):
-                rows = pl.ds(PIECE * piece, PIECE)
-                arrived(near_in.at[step, group, side, rows], near_recv_sem.at[step, group, side, piece])
-        share(step + 1, group, near_in[step, group, 0] + near_in[step, group, 1])
+        def value_of():
+            for piece in range(PIECES):
+                for side in range(2):
+                    rows = pl.ds(PIECE * piece, PIECE)
+                    arrived(near_in.at[step, group, side, rows], near_recv_sem.at[step, group, side, piece])
+            return near_in[step, group, 0] + near_in[step, group, 1]
+
+        share(step + 1, group, value_of)
+
+    def take_first(group):
+        def value_of():
+            arrived(incoming.at[group], first_recv_sem.at[group])
+            return pack(incoming.at[group], 0)
+
+        share(0, group, value_of)
 
     def send_last(group, which, device):
         send(
@@ -236,8 +271,7 @@
         last_take(group) if step == STEPS - 1 else take_near(step, group)
 
     for group in range(GROUPS):
-        arrived(incoming.at[group], first_recv_sem.at[group])
-        share(0, group, pack(incoming.at[group], 0))
+        take_first(group)
         begin(0, group)
     send_far(0, 0)
     send_far(0, 1)
@@ -253,6 +287,11 @@
                 send_far(step + 1, group)
     for copy in sent:
         copy.wait_send()
+
+    @pl.when(jnp.logical_not(is_last))
+    def _():
+        for copy in sent_below:
+            copy.wait_send()
 
 
 def sweep(green_blocks, traces, sources):

time: 74.5 us -> 72.4 us (0.972)
  the two profiles are of different devices: /device:TPU:1 before, /device:TPU:7 now
where the time goes in v3:
time: 72.4 us; the launch traced here: 71 us
  Pallas kernels  69.5 us (96%)
  local copies, waits for them, and re-layouts  1.57 us (2%)
    pallas_call x1, Pallas kernels, sweep(): pl.pallas_call(kernel, out_shape=jax.ShapeDtypeStruct(traces.shape, F32),...  69.5 us
    unnamed x1, local copies, waits for them, and re-layouts  1.57 us

profile of v3, /device:TPU:7, one launch (start us, length us, event | category | flops | bytes accessed | tf_op | source)
XLA Modules:
  0.0 71.0 jit_solution(16047572500786772136)
XLA Ops:
  0.0 69.5 %sweep.1 = f32[1,2,64,256]{3,2,1,0:T(8,128)} custom-call(f32[1,2,2048,256]{3,2,1,0:T(8,128)} %green.1, f32[1,2,64,256]{3,2,1,0:T(8,128)} %traces.1, f32[1,2,64,256]{3,2,1,0:T(8,128)} %sources.1), custom_call_target="tpu_custom_call" | custom-call | tf_op jit(solution)/shard_map/sweep/pallas_call | solution.py:299
  69.5 1.6 %copy.5 = f32[1,2,64,256]{3,2,1,0:T(8,128)} copy(f32[1,2,64,256]{3,2,1,0:T(8,128)} %sweep.1) | data formatting | bytes 262144

commit v4 on v3

--- a/solution.py
+++ b/solution.py
@@ -111,11 +111,10 @@
 
     def convert(origin, slot):
         for part in range(2):
-            for half in range(2):
-                high, low = split(staged[origin, slot, part, pl.ds(128 * half, 128), :])
-                columns = pl.ds(256 * ((origin * 2 + part) * 2 + half), 256)
-                left[slot, pl.ds(0, 128), columns] = high
-                left[slot, pl.ds(128, 128), columns] = low
+            high, low = split(staged[origin, slot, part])
+            columns = pl.ds(256 * (origin * 2 + part), 256)
+            left[slot, pl.ds(0, 256), columns] = high
+            left[slot, pl.ds(256, 256), columns] = low
 
     for slot in range(CHIPS):
         local[slot].wait()
@@ -147,25 +146,24 @@
         value = (held if origin == 0 else partner_held)[step, group]
         turned = jnp.where(real_lanes, -pltpu.roll(value, 96, 1), pltpu.roll(value, 32, 1))
         for part, term in ((0, value), (1, turned)):
-            swapped = pltpu.roll(term, 64, 1)
-            quarters = (
-                jnp.where(low_lanes, term, 0.0), jnp.where(low_lanes, swapped, 0.0),
-                jnp.where(low_lanes, 0.0, swapped), jnp.where(low_lanes, 0.0, term),
-            )
-            for index, quarter in enumerate(quarters):
-                high, low = split(quarter)
-                rows = pl.ds(256 * ((origin * 2 + part) * 2) + 128 * index, 128)
-                right[group, rows, pl.ds(0, 128)] = high
-                right[group, rows, pl.ds(128, 128)] = low
+            high = term.astype(BF16).astype(F32)
+            low = term - high
+            rows = 256 * (origin * 2 + part)
+            first = jnp.where(low_lanes, high, pltpu.roll(low, 64, 1))
+            second = jnp.where(low_lanes, pltpu.roll(high, 64, 1), low)
+            right[group, pl.ds(rows, 128), :] = first.astype(BF16)
+            right[group, pl.ds(rows + 128, 128), :] = second.astype(BF16)
 
     def product(group, slot, depth=slice(None)):
         full = jnp.dot(left[slot, :, depth], right[group, depth, :], preferred_element_type=F32)
-        return (full[:128, :128] + full[:128, 128:]) + (full[128:, :128] + full[128:, 128:])
+        full = full[:256] + full[256:]
+        full = full + pltpu.roll(full, 64, 1)
+        return jnp.where(low_lanes, full[:128], full[128:])
 
     def begin(step, group):
         make_right(step, group, 0)
         for slot in (FAR_A, FAR_B) if step < STEPS - 1 else (FAR_B,):
-            begun[group, slot] = product(group, slot, slice(0, 1024))
+            begun[group, slot] = product(group, slot, slice(0, 512))
 
     def send_far(step, group):
         arrived(partner_held.at[step, group], share_recv_sem.at[step, group])
@@ -174,7 +172,7 @@
             last_products(group)
             return
         for slot, device in ((FAR_A, at(slab, ahead, other)), (FAR_B, at(slab, behind, other))):
-            far_out[step, group, slot] = begun[group, slot] + product(group, slot, slice(1024, 2048))
+            far_out[step, group, slot] = begun[group, slot] + product(group, slot, slice(512, 1024))
             for piece in range(PIECES):
                 rows = pl.ds(PIECE * piece, PIECE)
                 send(
@@ -225,7 +223,7 @@
 
     def last_products(group):
         forward, backward = at(slab, ahead), at(slab, behind, other)
-        far = begun[group, FAR_B] + product(group, FAR_B, slice(1024, 2048))
+        far = begun[group, FAR_B] + product(group, FAR_B, slice(512, 1024))
         last_out[group, LAST_FAR_A] = far[:64]
         send_last(group, LAST_FAR_A, forward)
         last_out[group, LAST_FAR_B] = far[64:]
@@ -303,8 +301,8 @@
         out_specs=pl.BlockSpec(memory_space=pltpu.VMEM),
         scratch_shapes=[
             pltpu.VMEM((2, CHIPS, 2, 256, 256), F32),
-            pltpu.VMEM((CHIPS, 256, 2048), BF16),
-            pltpu.VMEM((GROUPS, 2048, 256), BF16),
+            pltpu.VMEM((CHIPS, 512, 1024), BF16),
+            pltpu.VMEM((GROUPS, 1024, 128), BF16),
             pltpu.VMEM((2, 64, 256), F32),
             pltpu.VMEM((GROUPS, 2, 32, 256), F32),
             pltpu.VMEM((STEPS, GROUPS, 128, 128), F32),

time: 72.4 us -> 72.9 us (level); the launches traced: 71 us -> 72.8 us
  Pallas kernels: 69.5 us -> 71.2 us
    pallas_call x1, Pallas kernels: 69.5 us -> 71.2 us  [sweep(): pl.pallas_call(kernel, out_shape=jax.ShapeDtypeStruct(traces.shape, F32),...]
where the time goes in v4:
time: 72.9 us; the launch traced here: 72.8 us
  Pallas kernels  71.2 us (98%)
  local copies, waits for them, and re-layouts  1.57 us (2%)
    pallas_call x1, Pallas kernels, sweep(): pl.pallas_call(kernel, out_shape=jax.ShapeDtypeStruct(traces.shape, F32),...  71.2 us
    unnamed x1, local copies, waits for them, and re-layouts  1.57 us

profile of v4, /device:TPU:7, one launch (start us, length us, event | category | flops | bytes accessed | tf_op | source)
XLA Modules:
  0.0 72.8 jit_solution(2497590957914498129)
XLA Ops:
  0.0 71.2 %sweep.1 = f32[1,2,64,256]{3,2,1,0:T(8,128)} custom-call(f32[1,2,2048,256]{3,2,1,0:T(8,128)} %green.1, f32[1,2,64,256]{3,2,1,0:T(8,128)} %traces.1, f32[1,2,64,256]{3,2,1,0:T(8,128)} %sources.1), custom_call_target="tpu_custom_call" | custom-call | tf_op jit(solution)/shard_map/sweep/pallas_call | solution.py:297
  71.2 1.6 %copy.5 = f32[1,2,64,256]{3,2,1,0:T(8,128)} copy(f32[1,2,64,256]{3,2,1,0:T(8,128)} %sweep.1) | data formatting | bytes 262144

commit v5 on v3

--- a/solution.py
+++ b/solution.py
@@ -8,7 +8,7 @@
 STEPS = 4
 GROUPS = 2
 CHIPS = 4
-PIECES = 2
+PIECES = 4
 PIECE = 128 // PIECES
 MESH = pl.DeviceIdType.MESH
 F32 = jnp.float32

time: 72.4 us -> 72 us (level); the launches traced: 71 us -> 71.8 us
  Pallas kernels: 69.5 us -> 70.3 us
    pallas_call x1, Pallas kernels: 69.5 us -> 70.3 us  [sweep(): pl.pallas_call(kernel, out_shape=jax.ShapeDtypeStruct(traces.shape, F32),...]
where the time goes in v5:
time: 72 us; the launch traced here: 71.8 us
  Pallas kernels  70.3 us (98%)
  local copies, waits for them, and re-layouts  1.57 us (2%)
    pallas_call x1, Pallas kernels, sweep(): pl.pallas_call(kernel, out_shape=jax.ShapeDtypeStruct(traces.shape, F32),...  70.3 us
    unnamed x1, local copies, waits for them, and re-layouts  1.57 us

profile of v5, /device:TPU:7, one launch (start us, length us, event | category | flops | bytes accessed | tf_op | source)
XLA Modules:
  0.0 71.8 jit_solution(1556091882279504561)
XLA Ops:
  0.0 70.3 %sweep.1 = f32[1,2,64,256]{3,2,1,0:T(8,128)} custom-call(f32[1,2,2048,256]{3,2,1,0:T(8,128)} %green.1, f32[1,2,64,256]{3,2,1,0:T(8,128)} %traces.1, f32[1,2,64,256]{3,2,1,0:T(8,128)} %sources.1), custom_call_target="tpu_custom_call" | custom-call | tf_op jit(solution)/shard_map/sweep/pallas_call | solution.py:299
  70.3 1.6 %copy.5 = f32[1,2,64,256]{3,2,1,0:T(8,128)} copy(f32[1,2,64,256]{3,2,1,0:T(8,128)} %sweep.1) | data formatting | bytes 262144
